TPU v7x, 512 devices: a whole 4x8x8 slice. The times are simulated.
512 devices in a mesh: blk: 32 (over z, y_hi), col: 16 (over x, y_lo, core).
Axes of the slice: x: 4, y: 8 (y_hi: 4, y_lo: 2; y = y_hi * 2 + y_lo), z: 8, core: 2. Of those that a mesh axis runs over, the one named last changes fastest.
Arguments:
- amps: bfloat16 [32, 16, 2, 128, 128], P('blk', 'col'), may hold values from -6 to 6
- driver: float32 [32, 16, 2, 128, 128], P('blk', 'col')
- pattern: int32 [32, 16, 2, 32, 2], P('blk', 'col'), may hold values from -1 to 31, as said below
- domain: int32 [32, 16, 2], P('blk', 'col'), may hold values from 32 to 128
- virt_energy: float32 [32, 16, 2, 128], P('blk', 'col'), may hold values from 0.5 to 4
- pair_gap: float32 [32, 16, 2], P('blk', 'col'), may hold values from 0.5 to 2
- integrals: bfloat16 [32, 128, 128], P('col'), may hold values from -0.0625 to 0.0625
Outputs:
- new_amps: float32 [32, 16, 2, 128, 128], P('blk', 'col')
- resid_rms: float32 [], replicated
Inputs may be any that keep to these rules, and one draw needn't show every extreme that they name: `pattern`: about a third of the entries are -1; the others name integral tiles of all owners.
All inputs are finite; a program needn't handle non-finite values.
Results may differ from a plain program's by a relative error of at most 0.0003.
Values may be sent and summed in bfloat16 or wider, within the bound.
A program may use at most 64 MiB of HBM per device.

v0:
```python
import jax
import jax.numpy as jnp
from jax import lax
from jax.sharding import PartitionSpec as P


def broadcast(block, axis, owner):
    block = jnp.where(lax.axis_index(axis) == owner, block, jnp.zeros_like(block))
    return lax.psum(block, axis)


def from_behind(block, axis, distance):
    devices = range(lax.axis_size(axis))
    route = [((i - distance) % len(devices), i) for i in devices]
    return lax.ppermute(block, axis, route)


def per_device(amps, driver, pattern, domain, virt_energy, pair_gap, integrals):
    width = amps.shape[-1]
    per_block = amps.shape[2]
    rows = jnp.arange(width, dtype=jnp.int32)
    edge = (rows[None, :] < domain[0, 0][:, None]).astype(jnp.float32)
    mask = edge[:, :, None] * edge[:, None, :]
    held = amps[0, 0] * mask.astype(jnp.bfloat16)
    links = pattern[0, 0].reshape(per_block, -1)
    owners = lax.axis_size("col")
    owned = integrals.shape[0]
    empty = jnp.zeros((owners * owned, width, width), jnp.bfloat16)

    def collect(root, buffer):
        piece = broadcast(integrals, "col", root)
        return lax.dynamic_update_slice_in_dim(buffer, piece, root * owned, 0)

    table = lax.fori_loop(0, owners, collect, empty)

    def couple(total, piece, start):
        count = piece.shape[0]
        idx = lax.dynamic_slice_in_dim(links, start, count, 1)
        valid = (idx >= 0).astype(jnp.bfloat16)
        tiles = table[jnp.maximum(idx, 0)] * valid[:, :, None, None]
        return total + jnp.einsum("qab,pqbc->pac", piece, tiles, preferred_element_type=jnp.float32)

    zero_total = jnp.zeros((per_block, width, width), jnp.float32)
    cycle_size = lax.axis_size("blk")
    own_place = lax.axis_index("blk")

    def cycle_step(turn, carry):
        total, visit = carry
        source = (own_place - turn) % cycle_size
        total = couple(total, visit, source * per_block)
        visit = from_behind(visit, "blk", 1)
        return (total, visit)

    total, visit = lax.fori_loop(0, cycle_size - 1, cycle_step, (zero_total, held))
    last_source = (own_place - (cycle_size - 1)) % cycle_size
    coupled = couple(total, visit, last_source * per_block)
    resid = mask * (driver[0, 0] + coupled)
    energy = virt_energy[0, 0]
    denom = energy[:, :, None] + energy[:, None, :] + pair_gap[0, 0][:, None, None]
    new_amps = held.astype(jnp.float32) + resid / denom
    squares = lax.psum(jnp.sum(resid * resid), ("blk", "col"))
    entries = float(lax.axis_size("blk") * lax.axis_size("col") * per_block * width * width)
    resid_rms = jnp.sqrt(squares / entries)
    return (new_amps[None, None], resid_rms)


def solution(mesh):
    in_specs = (
        P("blk", "col", None, None, None),
        P("blk", "col", None, None, None),
        P("blk", "col", None, None, None),
        P("blk", "col", None),
        P("blk", "col", None, None),
        P("blk", "col", None),
        P("col", None, None),
    )
    out_specs = (P("blk", "col", None, None, None), P())
    return jax.shard_map(
        per_device, mesh=mesh, in_specs=in_specs, out_specs=out_specs, check_vma=False
    )
```

profile of v0, /device:TPU:1, one launch (start us, length us, event | category | flops | bytes accessed | tf_op | source)
XLA Modules:
  0.0 2400.1 jit_solution(14885880743146692005)
XLA Ops:
  9.1 1957.6 %while.31 = (s32[]{:T(128)}, bf16[32,128,128]{2,1,0:T(8,128)(2,1)S(1)}, bf16[2,128,128]{2,1,0:T(8,128)(2,1)S(1)}, s32[]{:T(128)}, u32[]{:T(128)}, /*index=5*/s32[]{:T(128)}, s32[]{:T(128)}, s32[]{:T(128)}) while((s32[]{:T(128)}, bf16[32,128,128]{2,1,0:T(8,128)(2,1)S(1)}, bf16[2,128,128]{2,1,0:T(8,128)(2,1)S(1)}, s32[]{:T(128)}, u32[]{:T(128)}, ...), condition=%wide.region_2.3_spmd, body=%wide.region_0.2_spmd.sunk | while | flops 65545 | bytes 655565 | solution.py:34
  9.8 126.6 %all-reduce.2.cloned.1.call-done = bf16[2,128,128]{2,1,0:T(8,128)(2,1)} async-done(((bf16[2,128,128]{2,1,0:T(8,128)(2,1)}), bf16[2,128,128]{2,1,0:T(8,128)(2,1)}) %all-reduce.2.cloned.1.call-update) | async-done | bytes 65552 | tf_op jit(solution)/shard_map/while/body/eval_jaxpr/psum | solution.py:9
  138.0 120.5 %all-reduce.2.cloned.1.call-done = bf16[2,128,128]{2,1,0:T(8,128)(2,1)} async-done(((bf16[2,128,128]{2,1,0:T(8,128)(2,1)}), bf16[2,128,128]{2,1,0:T(8,128)(2,1)}) %all-reduce.2.cloned.1.call-update) | async-done | bytes 65552 | tf_op jit(solution)/shard_map/while/body/eval_jaxpr/psum | solution.py:9
  260.2 120.5 %all-reduce.2.cloned.1.call-done = bf16[2,128,128]{2,1,0:T(8,128)(2,1)} async-done(((bf16[2,128,128]{2,1,0:T(8,128)(2,1)}), bf16[2,128,128]{2,1,0:T(8,128)(2,1)}) %all-reduce.2.cloned.1.call-update) | async-done | bytes 65552 | tf_op jit(solution)/shard_map/while/body/eval_jaxpr/psum | solution.py:9
  382.3 120.2 %all-reduce.2.cloned.1.call-done = bf16[2,128,128]{2,1,0:T(8,128)(2,1)} async-done(((bf16[2,128,128]{2,1,0:T(8,128)(2,1)}), bf16[2,128,128]{2,1,0:T(8,128)(2,1)}) %all-reduce.2.cloned.1.call-update) | async-done | bytes 65552 | tf_op jit(solution)/shard_map/while/body/eval_jaxpr/psum | solution.py:9
  504.1 120.2 %all-reduce.2.cloned.1.call-done = bf16[2,128,128]{2,1,0:T(8,128)(2,1)} async-done(((bf16[2,128,128]{2,1,0:T(8,128)(2,1)}), bf16[2,128,128]{2,1,0:T(8,128)(2,1)}) %all-reduce.2.cloned.1.call-update) | async-done | bytes 65552 | tf_op jit(solution)/shard_map/while/body/eval_jaxpr/psum | solution.py:9
  625.9 120.2 %all-reduce.2.cloned.1.call-done = bf16[2,128,128]{2,1,0:T(8,128)(2,1)} async-done(((bf16[2,128,128]{2,1,0:T(8,128)(2,1)}), bf16[2,128,128]{2,1,0:T(8,128)(2,1)}) %all-reduce.2.cloned.1.call-update) | async-done | bytes 65552 | tf_op jit(solution)/shard_map/while/body/eval_jaxpr/psum | solution.py:9
  747.8 120.5 %all-reduce.2.cloned.1.call-done = bf16[2,128,128]{2,1,0:T(8,128)(2,1)} async-done(((bf16[2,128,128]{2,1,0:T(8,128)(2,1)}), bf16[2,128,128]{2,1,0:T(8,128)(2,1)}) %all-reduce.2.cloned.1.call-update) | async-done | bytes 65552 | tf_op jit(solution)/shard_map/while/body/eval_jaxpr/psum | solution.py:9
  869.9 120.5 %all-reduce.2.cloned.1.call-done = bf16[2,128,128]{2,1,0:T(8,128)(2,1)} async-done(((bf16[2,128,128]{2,1,0:T(8,128)(2,1)}), bf16[2,128,128]{2,1,0:T(8,128)(2,1)}) %all-reduce.2.cloned.1.call-update) | async-done | bytes 65552 | tf_op jit(solution)/shard_map/while/body/eval_jaxpr/psum | solution.py:9
  992.0 120.5 %all-reduce.2.cloned.1.call-done = bf16[2,128,128]{2,1,0:T(8,128)(2,1)} async-done(((bf16[2,128,128]{2,1,0:T(8,128)(2,1)}), bf16[2,128,128]{2,1,0:T(8,128)(2,1)}) %all-reduce.2.cloned.1.call-update) | async-done | bytes 65552 | tf_op jit(solution)/shard_map/while/body/eval_jaxpr/psum | solution.py:9
  1114.1 120.2 %all-reduce.2.cloned.1.call-done = bf16[2,128,128]{2,1,0:T(8,128)(2,1)} async-done(((bf16[2,128,128]{2,1,0:T(8,128)(2,1)}), bf16[2,128,128]{2,1,0:T(8,128)(2,1)}) %all-reduce.2.cloned.1.call-update) | async-done | bytes 65552 | tf_op jit(solution)/shard_map/while/body/eval_jaxpr/psum | solution.py:9
  1235.9 120.5 %all-reduce.2.cloned.1.call-done = bf16[2,128,128]{2,1,0:T(8,128)(2,1)} async-done(((bf16[2,128,128]{2,1,0:T(8,128)(2,1)}), bf16[2,128,128]{2,1,0:T(8,128)(2,1)}) %all-reduce.2.cloned.1.call-update) | async-done | bytes 65552 | tf_op jit(solution)/shard_map/while/body/eval_jaxpr/psum | solution.py:9
  1358.1 120.2 %all-reduce.2.cloned.1.call-done = bf16[2,128,128]{2,1,0:T(8,128)(2,1)} async-done(((bf16[2,128,128]{2,1,0:T(8,128)(2,1)}), bf16[2,128,128]{2,1,0:T(8,128)(2,1)}) %all-reduce.2.cloned.1.call-update) | async-done | bytes 65552 | tf_op jit(solution)/shard_map/while/body/eval_jaxpr/psum | solution.py:9
  1479.9 120.5 %all-reduce.2.cloned.1.call-done = bf16[2,128,128]{2,1,0:T(8,128)(2,1)} async-done(((bf16[2,128,128]{2,1,0:T(8,128)(2,1)}), bf16[2,128,128]{2,1,0:T(8,128)(2,1)}) %all-reduce.2.cloned.1.call-update) | async-done | bytes 65552 | tf_op jit(solution)/shard_map/while/body/eval_jaxpr/psum | solution.py:9
  1602.0 120.2 %all-reduce.2.cloned.1.call-done = bf16[2,128,128]{2,1,0:T(8,128)(2,1)} async-done(((bf16[2,128,128]{2,1,0:T(8,128)(2,1)}), bf16[2,128,128]{2,1,0:T(8,128)(2,1)}) %all-reduce.2.cloned.1.call-update) | async-done | bytes 65552 | tf_op jit(solution)/shard_map/while/body/eval_jaxpr/psum | solution.py:9
  1723.8 120.2 %all-reduce.2.cloned.1.call-done = bf16[2,128,128]{2,1,0:T(8,128)(2,1)} async-done(((bf16[2,128,128]{2,1,0:T(8,128)(2,1)}), bf16[2,128,128]{2,1,0:T(8,128)(2,1)}) %all-reduce.2.cloned.1.call-update) | async-done | bytes 65552 | tf_op jit(solution)/shard_map/while/body/eval_jaxpr/psum | solution.py:9
  1845.6 120.2 %all-reduce.2.cloned.1.call-done = bf16[2,128,128]{2,1,0:T(8,128)(2,1)} async-done(((bf16[2,128,128]{2,1,0:T(8,128)(2,1)}), bf16[2,128,128]{2,1,0:T(8,128)(2,1)}) %all-reduce.2.cloned.1.call-update) | async-done | bytes 65552 | tf_op jit(solution)/shard_map/while/body/eval_jaxpr/psum | solution.py:9
  1969.2 291.7 %while.32 = (s32[]{:T(128)}, f32[2,128,128]{1,2,0:T(8,128)S(1)}, bf16[2,128,128]{2,1,0:T(8,128)(2,1)S(1)}, s32[]{:T(128)}, s32[2,64]{1,0:T(2,128)S(1)}, /*index=...) while((s32[]{:T(128)}, f32[2,128,128]{1,2,0:T(8,128)S(1)}, ...), condition=%wide.region_4.5_spmd.clone, body=%wide.region_3.4_spmd.clone.sunk | while | flops 16909344 | bytes 1380822 | solution.py:54
  2000.4 6.8 collective-permute-done
  2019.6 6.1 collective-permute-done
  2038.0 6.5 collective-permute-done
  2056.9 6.1 collective-permute-done
  2084.7 6.6 collective-permute-done
  2094.5 6.8 collective-permute-done
  2132.1 7.0 collective-permute-done
  2151.4 6.1 collective-permute-done
  2179.1 6.6 collective-permute-done
  2189.0 6.8 collective-permute-done
  2217.3 6.1 collective-permute-done
  2226.6 6.6 collective-permute-done
  2236.3 6.2 collective-permute-done
  2263.3 128.4 %psum.18 = f32[]{:T(128)} all-reduce(f32[]{:T(128)} %get-tuple-element.280), channel_id=1, replica_groups=mesh['blk'=32,'col'=16] {'blk','col'}, use_global_device_ids=true, to_apply=%region_6.7 | all-reduce | flops 1 | bytes 8 | tf_op jit(solution)/shard_map/psum | solution.py:61
  (392 shorter events, 237.4 us)
Async XLA Ops:
  9.1 127.3 %all-reduce.2.cloned.1.call-start = ((), (), s32[]{:S(2)}) async-start(), calls=%async_computation | async-start | bytes 131072 | tf_op jit(solution)/shard_map/while/body/eval_jaxpr/psum | solution.py:9
  137.3 121.3 %all-reduce.2.cloned.1.call-start = ((), (), s32[]{:S(2)}) async-start(), calls=%async_computation | async-start | bytes 131072 | tf_op jit(solution)/shard_map/while/body/eval_jaxpr/psum | solution.py:9
  259.4 121.3 %all-reduce.2.cloned.1.call-start = ((), (), s32[]{:S(2)}) async-start(), calls=%async_computation | async-start | bytes 131072 | tf_op jit(solution)/shard_map/while/body/eval_jaxpr/psum | solution.py:9
  381.5 120.9 %all-reduce.2.cloned.1.call-start = ((), (), s32[]{:S(2)}) async-start(), calls=%async_computation | async-start | bytes 131072 | tf_op jit(solution)/shard_map/while/body/eval_jaxpr/psum | solution.py:9
  503.4 121.0 %all-reduce.2.cloned.1.call-start = ((), (), s32[]{:S(2)}) async-start(), calls=%async_computation | async-start | bytes 131072 | tf_op jit(solution)/shard_map/while/body/eval_jaxpr/psum | solution.py:9
  625.2 120.9 %all-reduce.2.cloned.1.call-start = ((), (), s32[]{:S(2)}) async-start(), calls=%async_computation | async-start | bytes 131072 | tf_op jit(solution)/shard_map/while/body/eval_jaxpr/psum | solution.py:9
  747.0 121.3 %all-reduce.2.cloned.1.call-start = ((), (), s32[]{:S(2)}) async-start(), calls=%async_computation | async-start | bytes 131072 | tf_op jit(solution)/shard_map/while/body/eval_jaxpr/psum | solution.py:9
  869.1 121.3 %all-reduce.2.cloned.1.call-start = ((), (), s32[]{:S(2)}) async-start(), calls=%async_computation | async-start | bytes 131072 | tf_op jit(solution)/shard_map/while/body/eval_jaxpr/psum | solution.py:9
  991.3 121.3 %all-reduce.2.cloned.1.call-start = ((), (), s32[]{:S(2)}) async-start(), calls=%async_computation | async-start | bytes 131072 | tf_op jit(solution)/shard_map/while/body/eval_jaxpr/psum | solution.py:9
  1113.4 121.0 %all-reduce.2.cloned.1.call-start = ((), (), s32[]{:S(2)}) async-start(), calls=%async_computation | async-start | bytes 131072 | tf_op jit(solution)/shard_map/while/body/eval_jaxpr/psum | solution.py:9
  1235.2 121.3 %all-reduce.2.cloned.1.call-start = ((), (), s32[]{:S(2)}) async-start(), calls=%async_computation | async-start | bytes 131072 | tf_op jit(solution)/shard_map/while/body/eval_jaxpr/psum | solution.py:9
  1357.3 120.9 %all-reduce.2.cloned.1.call-start = ((), (), s32[]{:S(2)}) async-start(), calls=%async_computation | async-start | bytes 131072 | tf_op jit(solution)/shard_map/while/body/eval_jaxpr/psum | solution.py:9
  1479.1 121.3 %all-reduce.2.cloned.1.call-start = ((), (), s32[]{:S(2)}) async-start(), calls=%async_computation | async-start | bytes 131072 | tf_op jit(solution)/shard_map/while/body/eval_jaxpr/psum | solution.py:9
  1601.3 120.9 %all-reduce.2.cloned.1.call-start = ((), (), s32[]{:S(2)}) async-start(), calls=%async_computation | async-start | bytes 131072 | tf_op jit(solution)/shard_map/while/body/eval_jaxpr/psum | solution.py:9
  1723.1 121.0 %all-reduce.2.cloned.1.call-start = ((), (), s32[]{:S(2)}) async-start(), calls=%async_computation | async-start | bytes 131072 | tf_op jit(solution)/shard_map/while/body/eval_jaxpr/psum | solution.py:9
  1844.9 120.9 %all-reduce.2.cloned.1.call-start = ((), (), s32[]{:S(2)}) async-start(), calls=%async_computation | async-start | bytes 131072 | tf_op jit(solution)/shard_map/while/body/eval_jaxpr/psum | solution.py:9
  1969.3 9.5 collective-permute-start
  1978.8 9.2 collective-permute-start
  1997.2 9.9 collective-permute-start
  2007.2 9.2 collective-permute-start
  2016.4 9.2 collective-permute-start
  2034.8 9.7 collective-permute-start
  2053.8 9.3 collective-permute-start
  2081.5 9.8 collective-permute-start
  2091.3 9.9 collective-permute-start
  2128.9 10.1 collective-permute-start
  2148.3 9.3 collective-permute-start
  2176.0 9.8 collective-permute-start
  2185.8 9.9 collective-permute-start
  2214.2 9.2 collective-permute-start
  2223.4 9.8 collective-permute-start
  2233.2 9.3 collective-permute-start
  (22 other events, 434.4 us)
Sparse Core Ops, SparseCore 0:
  13.4 123.0 all-reduce.1
  141.6 116.9 all-reduce.1
  263.7 116.9 all-reduce.1
  385.5 116.9 all-reduce.1
  507.3 116.9 all-reduce.1
  629.2 116.9 all-reduce.1
  751.3 116.9 all-reduce.1
  873.4 116.9 all-reduce.1
  995.5 116.9 all-reduce.1
  1117.4 116.9 all-reduce.1
  1239.5 116.9 all-reduce.1
  1361.3 116.9 all-reduce.1
  1483.4 116.9 all-reduce.1
  1605.3 116.9 all-reduce.1
  1727.1 116.9 all-reduce.1
  1848.9 116.9 all-reduce.1
where the time goes:
time: 2400 us
  waiting for transfers between devices  2120 us (88%)
  blocking collectives  128 us (5%)
  starting transfers between devices  61.1 us (3%)
  local copies, waits for them, and re-layouts  43.6 us (2%)
    psum x16, waiting for transfers between devices, broadcast(): return lax.psum(block, axis)  1930 us
    ppermute x31, waiting for transfers between devices, from_behind(): return lax.ppermute(block, axis, route)  192 us
    psum x1, blocking collectives, per_device(): squares = lax.psum(jnp.sum(resid * resid), ('blk', 'col'))  128 us
    ppermute x31, starting transfers between devices, from_behind(): return lax.ppermute(block, axis, route)  60.5 us
  transfers between devices with their start and end apart: 47, of which 47 were waited for; matrix products, arithmetic and copies ran while one was open for 2% of the time, Pallas kernels for 0%

commit v1 on v0

v1 whole, which is shorter than its diff:
```python
import functools

import jax
import jax.numpy as jnp
from jax import lax
from jax.experimental import pallas as pl
from jax.experimental.pallas import tpu as pltpu
from jax.sharding import PartitionSpec as P

MESH = pl.DeviceIdType.MESH
NY = 4
NL = 2
NC = 2
PEERS = 8


def far_first(n):
    return sorted(range(1, n), key=lambda d: -min(d, n - d))


def near_first(n):
    return sorted(range(1, n), key=lambda d: min(d, n - d))


def kernel(
    nz,
    nx,
    domain,
    pattern,
    amps,
    driver,
    integrals,
    resid_out,
    total_out,
    amps_v,
    held,
    driver_v,
    table,
    h,
    ints,
    idx,
    drv,
    y_a,
    y_b,
    acc,
    back,
    home,
    parts,
    local_sem,
    z_send,
    z_recv,
    y_send,
    y_recv,
    t_send,
    t_recv,
    r_send,
    r_recv,
    m_send,
    m_recv,
):
    f32 = jnp.float32
    width = held.shape[-1]
    rows = width // nz
    nk = table.shape[0] * 2
    blk = lax.axis_index("blk")
    col = lax.axis_index("col")
    z, yh = blk // NY, blk % NY
    x, yl, core = col // (NL * NC), (col // NC) % NL, col % NC

    def at_z(d):
        return (((z + d) % nz) * NY + yh, col)

    def at_yh(d):
        return (z * NY + (yh + d) % NY, col)

    def at_y(d):
        place = (yh * NL + yl + d) % (NY * NL)
        return (z * NY + place // NL, (x * NL + place % NL) * NC + core)

    def at_xc(d):
        place = (x * NC + core + d) % (nx * NC)
        return (blk, ((place // NC) * NL + yl) * NC + place % NC)

    def at_x(d):
        return (blk, (((x + d) % nx) * NL + yl) * NC + core)

    over = (blk, (x * NL + 1 - yl) * NC + core)
    sibling = (blk, (x * NL + yl) * NC + 1 - core)

    barrier = pltpu.get_barrier_semaphore()
    groups = ((at_z, nz), (at_y, NY * NL), (at_xc, nx * NC))
    for where_to, n in groups:
        for d in far_first(n):
            pl.semaphore_signal(barrier, inc=1, device_id=where_to(d), device_id_type=MESH)

    get_amps = pltpu.make_async_copy(amps, amps_v, local_sem.at[0])
    get_amps.start()
    get_tiles = []
    for j in range(2):
        get = pltpu.make_async_copy(
            integrals.at[j], table.at[col, :, pl.ds(j * width, width)], local_sem.at[1 + j]
        )
        get.start()
        get_tiles.append(get)
    get_driver = pltpu.make_async_copy(driver, driver_v, local_sem.at[3])
    get_driver.start()

    ints[z] = jnp.zeros(ints.shape[1:], jnp.int32)
    lane = lax.broadcasted_iota(jnp.int32, (pattern.shape[1], width), 1)
    sub = lax.broadcasted_iota(jnp.int32, (pattern.shape[1], width), 0)
    for p in range(2):
        both = jnp.where(
            lane % 2 == 0,
            jnp.broadcast_to(pattern[p, :, 0:1], lane.shape),
            jnp.broadcast_to(pattern[p, :, 1:2], lane.shape),
        )
        both = jnp.where(both < 0, nk, both)
        row = jnp.sum(jnp.where(sub == lane // 2, both, 0), axis=0, keepdims=True)
        ints[z, p : p + 1, :] = row
        ints[z, 2 + p : 3 + p, :] = jnp.full((1, width), domain[0, 0, p], jnp.int32)

    get_amps.wait()
    across = lax.broadcasted_iota(jnp.int32, (width, width), 1)
    down = lax.broadcasted_iota(jnp.int32, (width, width), 0)
    for q in range(2):
        inside = (across < domain[0, 0, q]) & (down < domain[0, 0, q])
        held[q] = jnp.where(inside, amps_v[q].astype(f32), 0.0).astype(jnp.bfloat16)
    mine = pl.ds(pl.multiple_of(z * rows, rows), rows)
    for q in range(2):
        h[0, z, q] = held[q, mine, :]
    for get in get_tiles:
        get.wait()
    pl.semaphore_wait(barrier, sum(n - 1 for _, n in groups))

    sends = []

    def send(src, dst, ssem, rsem, where_to):
        copy = pltpu.make_async_remote_copy(
            src_ref=src, dst_ref=dst, send_sem=ssem, recv_sem=rsem,
            device_id=where_to, device_id_type=MESH,
        )
        copy.start()
        sends.append(copy)

    def arrived(ref, ssem, rsem):
        pltpu.make_async_remote_copy(
            src_ref=ref, dst_ref=ref, send_sem=ssem, recv_sem=rsem,
            device_id=sibling, device_id_type=MESH,
        ).wait_recv()

    def their_rows(d):
        return pl.ds(pl.multiple_of(((z + d) % nz) * rows, rows), rows)

    for d in far_first(nz):
        send(held.at[:, their_rows(d), :], h.at[0, z], z_send.at[0, d], z_recv.at[0, d], at_z(d))

    def piece_out(d):
        zz = (z - d + nz) % nz
        send(h.at[0, zz], h.at[1, zz], y_send.at[0, d], y_recv.at[0, d], at_yh(1))
        send(h.at[0, zz], h.at[3, zz], y_send.at[1, d], y_recv.at[1, d], at_yh(NY - 1))

    def piece_from_z(d):
        zz = (z - d + nz) % nz
        arrived(h.at[0, zz], z_send.at[0, d], z_recv.at[0, d])
        piece_out(d)

    def piece_relay(d):
        zz = (z - d + nz) % nz
        arrived(h.at[1, zz], y_send.at[0, d], y_recv.at[0, d])
        send(h.at[1, zz, 0], h.at[2, zz, 0], y_send.at[2, d], y_recv.at[2, d], at_yh(1))
        arrived(h.at[3, zz], y_send.at[1, d], y_recv.at[1, d])
        send(h.at[3, zz, 1], h.at[2, zz, 1], y_send.at[3, d], y_recv.at[3, d], at_yh(NY - 1))

    def unit(dx, other):
        lo = 1 - yl if other else yl
        return table.at[(((x - dx + nx) % nx) * NL + lo) * NC + core]

    def unit_of_sibling(dx, other):
        lo = 1 - yl if other else yl
        return table.at[(((x - dx + nx) % nx) * NL + lo) * NC + 1 - core]

    half = width // 2
    def unit_along_x(other):
        base = 4 if other else 0
        send(unit(0, other), unit(0, other), t_send.at[base], t_recv.at[base], at_x(1))
        send(unit(0, other), unit(0, other), t_send.at[base + 1], t_recv.at[base + 1], at_x(nx - 1))

    def to_sibling(ref, n):
        send(ref, ref, t_send.at[n], t_recv.at[n], sibling)

    def unit_near(other):
        base = 4 if other else 0
        side = 15 if other else 10
        up, down_ = unit(1, other), unit(nx - 1, other)
        arrived(up, t_send.at[base], t_recv.at[base])
        first = up.at[pl.ds(0, half), :]
        send(first, first, t_send.at[base + 2], t_recv.at[base + 2], at_x(1))
        arrived(down_, t_send.at[base + 1], t_recv.at[base + 1])
        second = down_.at[pl.ds(half, half), :]
        send(second, second, t_send.at[base + 3], t_recv.at[base + 3], at_x(nx - 1))
        to_sibling(up, side)
        to_sibling(down_, side + 1)

    def unit_far(other):
        base = 4 if other else 0
        side = 17 if other else 12
        far = unit(2, other)
        for i in range(2):
            part = far.at[pl.ds(i * half, half), :]
            arrived(part, t_send.at[base + 2 + i], t_recv.at[base + 2 + i])
            to_sibling(part, side + i)

    piece_out(0)
    unit_along_x(False)
    send(unit(0, False), unit(0, False), t_send.at[8], t_recv.at[8], over)
    to_sibling(unit(0, False), 9)
    for d in far_first(nz):
        send(ints.at[z], ints.at[z], z_send.at[1, d], z_recv.at[1, d], at_z(d))
    get_driver.wait()
    for d in far_first(nz):
        send(driver_v.at[:, their_rows(d), :], drv.at[z], z_send.at[2, d], z_recv.at[2, d], at_z(d))
    for p in range(2):
        drv[z, p] = driver_v[p, mine, :]

    order = near_first(nz)
    for d in order[:4]:
        piece_from_z(d)
    piece_relay(0)
    unit_near(False)
    arrived(unit(0, True), t_send.at[8], t_recv.at[8])
    unit_along_x(True)
    to_sibling(unit(0, True), 14)
    for d in order[4:6]:
        piece_from_z(d)
    for d in order[:2]:
        piece_relay(d)
    for d in order[6:]:
        piece_from_z(d)
    for d in order[2:4]:
        piece_relay(d)
    unit_far(False)
    for d in order[4:6]:
        piece_relay(d)
    unit_near(True)
    for d in order[6:]:
        piece_relay(d)

    for d in order:
        arrived(ints.at[(z - d + nz) % nz], z_send.at[1, d], z_recv.at[1, d])
    get_idx = pltpu.make_async_copy(ints, idx, local_sem.at[4])
    get_idx.start()
    acc[...] = jnp.zeros_like(acc)
    y_a[nk] = jnp.zeros(y_a.shape[1:], f32)
    y_b[nk] = jnp.zeros(y_b.shape[1:], f32)
    unit_far(True)

    arrived(unit_of_sibling(0, False), t_send.at[9], t_recv.at[9])
    arrived(unit_of_sibling(0, True), t_send.at[14], t_recv.at[14])
    for other in (False, True):
        side = 15 if other else 10
        arrived(unit_of_sibling(1, other), t_send.at[side], t_recv.at[side])
        arrived(unit_of_sibling(nx - 1, other), t_send.at[side + 1], t_recv.at[side + 1])
        far = unit_of_sibling(2, other)
        for i in range(2):
            arrived(far.at[pl.ds(i * half, half), :], t_send.at[side + 2 + i], t_recv.at[side + 2 + i])
    get_idx.wait()

    def couple(dy, y):
        lhs = h[dy].reshape(nz * 2 * rows, width)
        for o in range(table.shape[0]):
            both = jnp.dot(lhs, table[o], preferred_element_type=f32)
            y[2 * o] = both[:, :width].reshape(nz * 2, rows, width)
            y[2 * o + 1] = both[:, width:].reshape(nz * 2, rows, width)
        behind = ((yh - dy + NY) % NY) * 2

        def add_up(g, carry):
            zo, p = g // 2, g % 2
            total = acc[g]
            for zs in range(nz):
                for q in range(2):
                    k = idx[zo, p, zs * NY * 2 + behind + q]
                    total = total + y[k, zs * 2 + q]
            acc[g] = total
            return carry

        lax.fori_loop(0, nz * 2, add_up, 0)

    couple(0, y_a)
    couple(1, y_b)
    couple(3, y_a)
    for d in range(nz):
        zz = (z - d + nz) % nz
        for i in range(2):
            arrived(h.at[2, zz, i], y_send.at[2 + i, d], y_recv.at[2 + i, d])
    couple(2, y_b)

    for d in order:
        arrived(drv.at[(z - d + nz) % nz], z_send.at[2, d], z_recv.at[2, d])
    below = lax.broadcasted_iota(jnp.int32, (rows, width), 0) + z * rows
    aside = lax.broadcasted_iota(jnp.int32, (rows, width), 1)
    squares = jnp.zeros((rows, width), f32)
    for zo in range(nz):
        for p in range(2):
            limit = idx[zo, 2 + p, 0]
            inside = (below < limit) & (aside < limit)
            value = jnp.where(inside, drv[zo, p] + acc[zo * 2 + p], 0.0)
            back[zo, p] = value
            squares = squares + value * value
    squares = jnp.sum(squares.reshape(rows // 8, 8, width), axis=0)

    def stage_out(i, place, where_to, n, value):
        parts[i, place] = value
        for d in far_first(n):
            send(parts.at[i, place], parts.at[i, place], m_send.at[i, d], m_recv.at[i, d], where_to(d))

    def stage_in(i, place, n):
        for d in near_first(n):
            arrived(parts.at[i, (place - d + n) % n], m_send.at[i, d], m_recv.at[i, d])
        total = parts[i, 0]
        for j in range(1, n):
            total = total + parts[i, j]
        return total

    xc, yy = x * NC + core, yh * NL + yl
    stage_out(0, xc, at_xc, nx * NC, squares)
    for d in far_first(nz):
        send(back.at[(z + d) % nz], home.at[:, mine, :], r_send.at[d], r_recv.at[d], at_z(d))
    for p in range(2):
        home[p, mine, :] = back[z, p]
    total = stage_in(0, xc, nx * NC)
    stage_out(1, yy, at_y, NY * NL, total)
    total = stage_in(1, yy, NY * NL)
    stage_out(2, z, at_z, nz, total)
    for d in order:
        theirs = pl.ds(pl.multiple_of(((z - d + nz) % nz) * rows, rows), rows)
        arrived(home.at[:, theirs, :], r_send.at[d], r_recv.at[d])
    resid_out[...] = home[...]
    total = stage_in(2, z, nz)
    total_out[...] = jnp.full(total_out.shape, jnp.sum(total), f32)
    for copy in sends:
        copy.wait_send()


def per_device(amps, driver, pattern, domain, virt_energy, pair_gap, integrals):
    width = amps.shape[-1]
    per_block = amps.shape[2]
    nz = lax.axis_size("blk") // NY
    nx = lax.axis_size("col") // (NL * NC)
    rows_of = width // nz
    owners = lax.axis_size("col")
    nk = owners * integrals.shape[0]
    dma = pltpu.SemaphoreType.DMA
    anywhere = pl.BlockSpec(memory_space=pl.ANY)
    in_vmem = pl.BlockSpec(memory_space=pltpu.VMEM)
    tile = (width, width)
    resid, total = pl.pallas_call(
        functools.partial(kernel, nz, nx),
        out_shape=(
            jax.ShapeDtypeStruct((per_block, *tile), jnp.float32),
            jax.ShapeDtypeStruct((8, width), jnp.float32),
        ),
        in_specs=[pl.BlockSpec(memory_space=pltpu.SMEM), in_vmem, anywhere, anywhere, anywhere],
        out_specs=(in_vmem, in_vmem),
        scratch_shapes=[
            pltpu.VMEM((2, *tile), jnp.bfloat16),
            pltpu.VMEM((2, *tile), jnp.bfloat16),
            pltpu.VMEM((2, *tile), jnp.float32),
            pltpu.VMEM((owners, width, 2 * width), jnp.bfloat16),
            pltpu.VMEM((NY, nz, 2, rows_of, width), jnp.bfloat16),
            pltpu.VMEM((nz, 8, width), jnp.int32),
            pltpu.SMEM((nz, 8, width), jnp.int32),
            pltpu.VMEM((nz, 2, rows_of, width), jnp.float32),
            pltpu.VMEM((nk + 1, nz * 2, rows_of, width), jnp.float32),
            pltpu.VMEM((nk + 1, nz * 2, rows_of, width), jnp.float32),
            pltpu.VMEM((nz * 2, rows_of, width), jnp.float32),
            pltpu.VMEM((nz, 2, rows_of, width), jnp.float32),
            pltpu.VMEM((2, *tile), jnp.float32),
            pltpu.VMEM((3, PEERS, 8, width), jnp.float32),
            dma((5,)),
            dma((3, nz)),
            dma((3, nz)),
            dma((4, nz)),
            dma((4, nz)),
            dma((19,)),
            dma((19,)),
            dma((nz,)),
            dma((nz,)),
            dma((3, PEERS)),
            dma((3, PEERS)),
        ],
        compiler_params=pltpu.CompilerParams(
            collective_id=0, has_side_effects=True, vmem_limit_bytes=32 * 1024 * 1024
        ),
    )(domain, pattern[0, 0], amps[0, 0], driver[0, 0], integrals)

    rows = jnp.arange(width, dtype=jnp.int32)
    edge = rows[None, :] < domain[0, 0][:, None]
    inside = edge[:, :, None] & edge[:, None, :]
    energy = virt_energy[0, 0]
    denom = energy[:, :, None] + energy[:, None, :] + pair_gap[0, 0][:, None, None]
    held = jnp.where(inside, amps[0, 0].astype(jnp.float32), 0.0)
    new_amps = held + resid / denom
    entries = float(lax.axis_size("blk") * owners * per_block * width * width)
    resid_rms = jnp.sqrt(total[0, 0] / entries)
    return (new_amps[None, None], resid_rms)


def solution(mesh):
    in_specs = (
        P("blk", "col", None, None, None),
        P("blk", "col", None, None, None),
        P("blk", "col", None, None, None),
        P("blk", "col", None),
        P("blk", "col", None, None),
        P("blk", "col", None),
        P("col", None, None),
    )
    out_specs = (P("blk", "col", None, None, None), P())
    return jax.shard_map(
        per_device, mesh=mesh, in_specs=in_specs, out_specs=out_specs, check_vma=False
    )
```

time: 2400 us -> 58.6 us (0.02)
  waiting for transfers between devices: 2120 us -> 0 us
  blocking collectives: 128 us -> 0 us
  starting transfers between devices: 61.1 us -> 0 us
  Pallas kernels: 0 us -> 50.4 us
  local copies, waits for them, and re-layouts: 43.6 us -> 4.5 us
    psum x16 -> x0, waiting for transfers between devices: 1930 us -> none  [broadcast(): return lax.psum(block, axis)]
    ppermute x31 -> x0, waiting for transfers between devices: 192 us -> none  [from_behind(): return lax.ppermute(block, axis, route)]
    psum x1 -> x0, blocking collectives: 128 us -> none  [per_device(): squares = lax.psum(jnp.sum(resid * resid), ('blk', 'col'))]
    ppermute x31 -> x0, starting transfers between devices: 60.5 us -> none  [from_behind(): return lax.ppermute(block, axis, route)]
    pallas_call x0 -> x1, Pallas kernels: none -> 50.4 us  [per_device(): pl.pallas_call(functools.partial(kernel, nz, nx), out_shape=(jax.ShapeDty...]
  transfers between devices with their start and end apart: 47 -> 0, of which waited for: 47 -> 0; matrix products, arithmetic and copies ran while one was open for 2% -> 0% of each run, Pallas kernels for 0% -> 0%
where the time goes in v1:
time: 58.6 us; the launch traced here: 58.3 us
  Pallas kernels  50.4 us (86%)
  local copies, waits for them, and re-layouts  4.5 us (8%)
  between operations  2.5 us (4%)
  other arithmetic  0.87 us (1%)
    pallas_call x1, Pallas kernels, per_device(): pl.pallas_call(functools.partial(kernel, nz, nx), out_shape=(jax.ShapeDty...  50.4 us
    unnamed x14, local copies, waits for them, and re-layouts  3.9 us

profile of v1, /device:TPU:1, one launch (start us, length us, event | category | flops | bytes accessed | tf_op | source)
XLA Modules:
  0.0 58.3 jit_solution(10938299395692991838)
XLA Ops:
  0.6 0.0 copy-start.3
  0.6 0.0 copy-start.5
  0.6 0.6 %copy-done.3 = s32[1,1,2]{2,1,0:T(1,128)S(1)} copy-done((s32[1,1,2]{2,1,0:T(1,128)S(1)}, s32[1,1,2]{2,1,0:T(1,128)}, u32[]{:S(2)}) %copy-start.3) | copy-done | bytes 32
  1.3 0.1 iota_compare_fusion
  1.4 0.0 copy-done.5
  1.4 0.1 copy.9.pattern
  1.5 0.0 copy-start
  1.5 0.8 %copy-done = bf16[1,1,2,128,128]{4,3,2,1,0:T(8,128)(2,1)S(1)} copy-done((bf16[1,1,2,128,128]{4,3,2,1,0:T(8,128)(2,1)S(1)}, bf16[1,1,2,128,128]{4,3,2,1,0:T(8,128)(2,1)}, u32[]{:S(2)}) %copy-start) | copy-done | bytes 65560
  2.3 0.0 copy-start.1
  2.3 0.9 %copy-done.1 = f32[1,1,2,128,128]{4,3,2,1,0:T(8,128)S(1)} copy-done((f32[1,1,2,128,128]{4,3,2,1,0:T(8,128)S(1)}, f32[1,1,2,128,128]{4,3,2,1,0:T(8,128)}, u32[]{:S(2)}) %copy-start.1) | copy-done | bytes 131096
  3.2 0.0 copy-start.2
  3.2 0.8 %copy-done.2 = bf16[2,128,128]{2,1,0:T(8,128)(2,1)S(1)} copy-done((bf16[2,128,128]{2,1,0:T(8,128)(2,1)S(1)}, bf16[2,128,128]{2,1,0:T(8,128)(2,1)}, u32[]{:S(2)}) %copy-start.2) | copy-done | bytes 65560
  4.0 50.4 %shard_map.86 = (f32[2,128,128]{2,1,0:T(8,128)S(1)}, f32[8,128]{1,0:T(8,128)S(1)}) custom-call(s32[1,1,2]{2,1,0:T(1,128)S(1)} %copy-done.3, s32[2,32,2]{2,1,0:T(8,128)S(1)} %copy.9.pattern, bf16[2,128,128]{2,1,0:T(8,128)(2,1)S(1)} %bitcast.10, f32[2,128,128]{2,1,0:T(8,128)S(1)} %bitcast.11, bf16[2,128,128]{2,1,0:T(8,128)(2,1)S(1)} %copy-done.2), custom_call_target="tpu_custom_call" | custom-call | tf_op jit(solution)/shard_map/pallas_call | solution.py:356
  54.5 0.5 slice.3
  55.7 0.0 copy-start.4
  55.7 0.0 copy-start.6
  55.7 0.7 %copy-done.4 = f32[1,1,2,128]{3,2,1,0:T(2,128)S(1)} copy-done((f32[1,1,2,128]{3,2,1,0:T(2,128)S(1)}, f32[1,1,2,128]{3,2,1,0:T(2,128)}, u32[]{:S(2)}) %copy-start.4) | copy-done | bytes 1048
  56.4 0.0 copy-done.6
  56.4 0.8 %add_bitcast_fusion = f32[1,1,2,128,128]{4,3,2,1,0:T(8,128)} fusion(f32[2,128,128]{2,1,0:T(8,128)S(1)} %get-tuple-element.4, f32[2]{0:T(128)S(1)} %bitcast.15, f32[2,128]{1,0:T(2,128)S(1)} %bitcast.13, pred[2,128]{1,0:T(4,128)(4,1)S(1)} %iota_compare_fusion, bf16[1,1,2,128,128]{4,3,2,1,0:T(8,128)(2,1)S(1)} %copy-done), kind=kLoop, calls=%fused_computation | loop fusion | flops 229376 | bytes 328968 | tf_op jit(solution)/shard_map/broadcast_in_dim | solution.py:405
Async XLA Ops:
  0.6 0.7 %copy-start.3 = (s32[1,1,2]{2,1,0:T(1,128)S(1)}, s32[1,1,2]{2,1,0:T(1,128)}, u32[]{:S(2)}) copy-start(s32[1,1,2]{2,1,0:T(1,128)} %domain.1) | copy-start | bytes 28
  0.6 0.7 %copy-start.5 = (s32[1,1,2,32,2]{3,4,2,1,0:T(2,128)S(1)}, s32[1,1,2,32,2]{3,4,2,1,0:T(2,128)}, u32[]{:S(2)}) copy-start(s32[1,1,2,32,2]{3,4,2,1,0:T(2,128)} %param.9) | copy-start | bytes 1540
  1.5 0.8 %copy-start = (bf16[1,1,2,128,128]{4,3,2,1,0:T(8,128)(2,1)S(1)}, bf16[1,1,2,128,128]{4,3,2,1,0:T(8,128)(2,1)}, u32[]{:S(2)}) copy-start(bf16[1,1,2,128,128]{4,3,2,1,0:T(8,128)(2,1)} %param.7) | copy-start | bytes 196612
  2.3 0.9 %copy-start.1 = (f32[1,1,2,128,128]{4,3,2,1,0:T(8,128)S(1)}, f32[1,1,2,128,128]{4,3,2,1,0:T(8,128)}, u32[]{:S(2)}) copy-start(f32[1,1,2,128,128]{4,3,2,1,0:T(8,128)} %param.8) | copy-start | bytes 393220
  3.2 0.8 %copy-start.2 = (bf16[2,128,128]{2,1,0:T(8,128)(2,1)S(1)}, bf16[2,128,128]{2,1,0:T(8,128)(2,1)}, u32[]{:S(2)}) copy-start(bf16[2,128,128]{2,1,0:T(8,128)(2,1)} %integrals.1) | copy-start | bytes 196612
  55.7 0.7 %copy-start.4 = (f32[1,1,2,128]{3,2,1,0:T(2,128)S(1)}, f32[1,1,2,128]{3,2,1,0:T(2,128)}, u32[]{:S(2)}) copy-start(f32[1,1,2,128]{3,2,1,0:T(2,128)} %param.11) | copy-start | bytes 3076
  55.7 0.7 %copy-start.6 = (f32[1,1,2]{2,1,0:T(1,128)S(1)}, f32[1,1,2]{2,1,0:T(1,128)}, u32[]{:S(2)}) copy-start(f32[1,1,2]{2,1,0:T(1,128)} %param.12) | copy-start | bytes 28

commit v2 on v1

v2 whole, which is shorter than its diff:
```python
import functools

import jax
import jax.numpy as jnp
from jax import lax
from jax.experimental import pallas as pl
from jax.experimental.pallas import tpu as pltpu
from jax.sharding import PartitionSpec as P

MESH = pl.DeviceIdType.MESH
NY = 4
NL = 2
NC = 2


def far_first(n):
    return sorted(range(1, n), key=lambda d: -min(d, n - d))


def near_first(n):
    return sorted(range(1, n), key=lambda d: min(d, n - d))


def kernel(
    nz,
    nx,
    entries,
    domain,
    pattern,
    amps,
    driver,
    energy,
    gap,
    integrals,
    amps_out,
    rms_out,
    domain_s,
    gap_s,
    pattern_v,
    energy_v,
    amps_v,
    held,
    driver_v,
    denom,
    table,
    h,
    ints,
    idx,
    drv,
    y_near,
    y_far,
    acc,
    back,
    home,
    parts,
    local_sem,
    z_send,
    z_recv,
    y_send,
    y_recv,
    t_send,
    t_recv,
    r_send,
    r_recv,
    m_send,
    m_recv,
):
    f32 = jnp.float32
    width = held.shape[-1]
    rows = width // nz
    nk = table.shape[0] * 2
    blk = lax.axis_index("blk")
    col = lax.axis_index("col")
    z, yh = blk // NY, blk % NY
    x, yl, core = col // (NL * NC), (col // NC) % NL, col % NC

    def at_z(d):
        return (((z + d) % nz) * NY + yh, col)

    def at_yh(d):
        return (z * NY + (yh + d) % NY, col)

    def at_y(d):
        place = (yh * NL + yl + d) % (NY * NL)
        return (z * NY + place // NL, (x * NL + place % NL) * NC + core)

    def at_x(d):
        return (blk, (((x + d) % nx) * NL + yl) * NC + core)

    def at_zc(d, e):
        return (((z + d) % nz) * NY + yh, (x * NL + yl) * NC + (core + e) % NC)

    over = (blk, (x * NL + 1 - yl) * NC + core)
    sibling = (blk, (x * NL + yl) * NC + 1 - core)
    zc_far = [(d, e) for d in far_first(nz) for e in range(NC)] + [(0, 1)]

    barrier = pltpu.get_barrier_semaphore()
    greeted = [at_zc(d, e) for d, e in zc_far]
    greeted += [at_y(d) for d in far_first(NY * NL)]
    greeted += [at_x(d) for d in far_first(nx)]
    for device in greeted:
        pl.semaphore_signal(barrier, inc=1, device_id=device, device_id_type=MESH)

    gets = []
    for src, dst in (
        (domain, domain_s),
        (amps, amps_v),
        (pattern, pattern_v),
        (integrals.at[0], table.at[col, :, pl.ds(0, width)]),
        (integrals.at[1], table.at[col, :, pl.ds(width, width)]),
        (driver, driver_v),
        (energy, energy_v),
        (gap, gap_s),
    ):
        get = pltpu.make_async_copy(src, dst, local_sem.at[len(gets)])
        get.start()
        gets.append(get)

    across = lax.broadcasted_iota(jnp.int32, (width, width), 1)
    down = lax.broadcasted_iota(jnp.int32, (width, width), 0)
    mine = pl.ds(pl.multiple_of(z * rows, rows), rows)
    gets[0].wait()
    gets[1].wait()
    for q in range(2):
        inside = (across < domain_s[0, 0, q]) & (down < domain_s[0, 0, q])
        held[q] = jnp.where(inside, amps_v[q].astype(f32), 0.0).astype(jnp.bfloat16)
    for q in range(2):
        h[0, 0, q] = held[q, mine, :]

    gets[2].wait()
    ints[z] = jnp.zeros(ints.shape[1:], jnp.int32)
    places = pattern_v.shape[-1]
    for p in range(2):
        tiles = pattern_v[p]
        ints[z, 2 * p : 2 * p + 2, 0:places] = jnp.where(tiles < 0, nk, tiles)
        ints[z, 4 + p : 5 + p, :] = jnp.full((1, width), domain_s[0, 0, p], jnp.int32)

    gets[3].wait()
    gets[4].wait()
    pl.semaphore_wait(barrier, len(greeted))

    sends = []

    def send(src, dst, ssem, rsem, where_to):
        copy = pltpu.make_async_remote_copy(
            src_ref=src, dst_ref=dst, send_sem=ssem, recv_sem=rsem,
            device_id=where_to, device_id_type=MESH,
        )
        copy.start()
        sends.append(copy)

    def arrived(ref, ssem, rsem):
        pltpu.make_async_remote_copy(
            src_ref=ref, dst_ref=ref, send_sem=ssem, recv_sem=rsem,
            device_id=sibling, device_id_type=MESH,
        ).wait_recv()

    def their_rows(d):
        return pl.ds(pl.multiple_of(((z + d) % nz) * rows, rows), rows)

    order = near_first(nz)
    slot = {d: i for i, d in enumerate([0] + order)}

    for d in far_first(nz):
        send(held.at[:, their_rows(d), :], h.at[slot[d], 0], z_send.at[0, d], z_recv.at[0, d], at_z(d))

    def piece_out(d):
        piece = h.at[slot[d], 0]
        for dy in (2, 1, 3):
            send(piece, h.at[slot[d], dy], y_send.at[d, dy], y_recv.at[d, dy], at_yh(dy))

    def piece_from_z(d):
        arrived(h.at[slot[d], 0], z_send.at[0, d], z_recv.at[0, d])
        piece_out(d)

    def owner(dx, other, far_core):
        lo = 1 - yl if other else yl
        return (((x - dx + nx) % nx) * NL + lo) * NC + (1 - core if far_core else core)

    def unit(dx, other, far_core=0):
        return table.at[owner(dx, other, far_core)]

    def kind(dx, other, far_core=0):
        return dx + nx * other + 2 * nx * far_core

    def unit_along_x(other):
        n = unit(0, other)
        for d in far_first(nx):
            send(n, n, t_send.at[kind(d, other)], t_recv.at[kind(d, other)], at_x(d))

    def unit_to_sibling(dx, other):
        n = unit(dx, other)
        send(n, n, t_send.at[kind(dx, other, 1)], t_recv.at[kind(dx, other, 1)], sibling)

    def unit_in(dx, other, far_core=0):
        n = kind(dx, other, far_core)
        arrived(unit(dx, other, far_core), t_send.at[n], t_recv.at[n])

    def unit_from_x(dx, other):
        unit_in(dx, other)
        unit_to_sibling(dx, other)

    send(unit(0, 0), unit(0, 0), t_send.at[kind(0, 1)], t_recv.at[kind(0, 1)], over)
    unit_along_x(0)
    piece_out(0)
    unit_to_sibling(0, 0)
    for d in far_first(nz):
        send(ints.at[z], ints.at[z], z_send.at[1, d], z_recv.at[1, d], at_z(d))
    gets[5].wait()
    for d in far_first(nz):
        send(driver_v.at[:, their_rows(d), :], drv.at[z], z_send.at[2, d], z_recv.at[2, d], at_z(d))
    for p in range(2):
        drv[z, p] = driver_v[p, mine, :]
    acc[...] = jnp.zeros_like(acc)
    y_near[nk] = jnp.zeros(y_near.shape[1:], f32)
    y_far[nk] = jnp.zeros(y_far.shape[1:], f32)

    for d in order[:4]:
        piece_from_z(d)
    unit_in(0, 1)
    unit_along_x(1)
    unit_to_sibling(0, 1)
    for d in order[4:6]:
        piece_from_z(d)
    for d in near_first(nx)[:2]:
        unit_from_x(d, 0)
    for d in order[6:]:
        piece_from_z(d)
    for d in near_first(nx)[2:]:
        unit_from_x(d, 0)

    for d in order:
        arrived(ints.at[(z - d + nz) % nz], z_send.at[1, d], z_recv.at[1, d])
    get_idx = pltpu.make_async_copy(ints, idx, local_sem.at[len(gets)])
    get_idx.start()
    gets[6].wait()
    gets[7].wait()
    for p in range(2):
        own = jnp.broadcast_to(energy_v[0, 0, p : p + 1, :], (width, width))
        turned = jnp.sum(jnp.where(across == down, own, 0.0), axis=1, keepdims=True)
        denom[p] = turned + own + gap_s[0, 0, p]
    for d in near_first(nx):
        unit_from_x(d, 1)
    get_idx.wait()

    def pieces_in(ds):
        for d in ds:
            for dy in (1, 3, 2):
                arrived(h.at[slot[d], dy], y_send.at[d, dy], y_recv.at[d, dy])

    def couple(ds, y, wait_units):
        first, count = slot[ds[0]], len(ds)
        lhs = h[first : first + count].reshape(count * NY * 2 * rows, width)
        for far_core in range(2):
            for other in range(2):
                for dx in [0] + near_first(nx):
                    if wait_units and far_core:
                        unit_in(dx, other, 1)
                    o = owner(dx, other, far_core)
                    both = jnp.dot(lhs, table[o], preferred_element_type=f32)
                    y[2 * o] = both[:, :width].reshape(count * NY * 2, rows, width)
                    y[2 * o + 1] = both[:, width:].reshape(count * NY * 2, rows, width)
        behind = [[((z - d + nz) % nz) * NY + (yh - dy + NY) % NY for dy in range(NY)] for d in ds]

        def add_up(g, carry):
            zo, p = g // 2, g % 2
            total = acc[g]
            for i in range(count):
                for dy in range(NY):
                    for q in range(2):
                        k = idx[zo, p * 2 + q, behind[i][dy]]
                        total = total + y[k, (i * NY + dy) * 2 + q]
            acc[g] = total
            return carry

        lax.fori_loop(0, nz * 2, add_up, 0)

    near = [0] + order[:4]
    pieces_in(near)
    couple(near, y_near, True)
    pieces_in(order[4:])
    couple(order[4:], y_far, False)

    for d in order:
        arrived(drv.at[(z - d + nz) % nz], z_send.at[2, d], z_recv.at[2, d])
    below = lax.broadcasted_iota(jnp.int32, (rows, width), 0) + z * rows
    aside = lax.broadcasted_iota(jnp.int32, (rows, width), 1)
    squares = jnp.zeros((rows, width), f32)
    for zo in range(nz):
        for p in range(2):
            limit = idx[zo, 4 + p, 0]
            inside = (below < limit) & (aside < limit)
            value = jnp.where(inside, drv[zo, p] + acc[zo * 2 + p], 0.0)
            back[zo, p] = value
            squares = squares + value * value
    squares = jnp.sum(squares, axis=0, keepdims=True)

    def stage_out(i, place, peers, value):
        parts[i, place] = value
        for j, device in enumerate(peers):
            send(parts.at[i, place], parts.at[i, place], m_send.at[i, j], m_recv.at[i, j], device)

    def stage_in(i, places):
        for j, place in reversed(list(enumerate(places))):
            arrived(parts.at[i, place], m_send.at[i, j], m_recv.at[i, j])
        total = parts[i, 0]
        for j in range(1, len(places) + 1):
            total = total + parts[i, j]
        return total

    yy, ny = yh * NL + yl, NY * NL
    stage_out(0, z * NC + core, [at_zc(d, e) for d, e in zc_far], squares)
    for d in far_first(nz):
        send(back.at[(z + d) % nz], home.at[:, mine, :], r_send.at[d], r_recv.at[d], at_z(d))
    for p in range(2):
        home[p, mine, :] = back[z, p]
    total = stage_in(0, [((z - d + nz) % nz) * NC + (core + e) % NC for d, e in zc_far])
    stage_out(1, yy, [at_y(d) for d in far_first(ny)], total)
    total = stage_in(1, [(yy - d + ny) % ny for d in far_first(ny)])
    stage_out(2, x, [at_x(d) for d in far_first(nx)], total)
    for d in order:
        theirs = pl.ds(pl.multiple_of(((z - d + nz) % nz) * rows, rows), rows)
        arrived(home.at[:, theirs, :], r_send.at[d], r_recv.at[d])
    for p in range(2):
        amps_out[p] = held[p].astype(f32) + home[p] / denom[p]
    total = stage_in(2, [(x - d + nx) % nx for d in far_first(nx)])
    rms_out[0, 0] = jnp.max(jnp.sqrt(jnp.full((8, width), jnp.sum(total) / entries, f32)))
    for copy in sends:
        copy.wait_send()


def per_device(amps, driver, pattern, domain, virt_energy, pair_gap, integrals):
    width = amps.shape[-1]
    per_block = amps.shape[2]
    nz = lax.axis_size("blk") // NY
    nx = lax.axis_size("col") // (NL * NC)
    rows_of = width // nz
    owners = lax.axis_size("col")
    nk = owners * integrals.shape[0]
    entries = float(lax.axis_size("blk") * owners * per_block * width * width)
    near = 5
    dma = pltpu.SemaphoreType.DMA
    in_hbm = pl.BlockSpec(memory_space=pltpu.HBM)
    tile = (width, width)
    new_amps, rms = pl.pallas_call(
        functools.partial(kernel, nz, nx, entries),
        out_shape=(
            jax.ShapeDtypeStruct((per_block, *tile), jnp.float32),
            jax.ShapeDtypeStruct((1, 1), jnp.float32),
        ),
        in_specs=[in_hbm] * 7,
        out_specs=(pl.BlockSpec(memory_space=pltpu.VMEM), pl.BlockSpec(memory_space=pltpu.SMEM)),
        scratch_shapes=[
            pltpu.SMEM((1, 1, 2), jnp.int32),
            pltpu.SMEM((1, 1, 2), jnp.float32),
            pltpu.VMEM((2, 2, pattern.shape[3]), jnp.int32),
            pltpu.VMEM((1, 1, 2, width), jnp.float32),
            pltpu.VMEM((2, *tile), jnp.bfloat16),
            pltpu.VMEM((2, *tile), jnp.bfloat16),
            pltpu.VMEM((2, *tile), jnp.float32),
            pltpu.VMEM((2, *tile), jnp.float32),
            pltpu.VMEM((owners, width, 2 * width), jnp.bfloat16),
            pltpu.VMEM((nz, NY, 2, rows_of, width), jnp.bfloat16),
            pltpu.VMEM((nz, 8, width), jnp.int32),
            pltpu.SMEM((nz, 8, width), jnp.int32),
            pltpu.VMEM((nz, 2, rows_of, width), jnp.float32),
            pltpu.VMEM((nk + 1, near * NY * 2, rows_of, width), jnp.float32),
            pltpu.VMEM((nk + 1, (nz - near) * NY * 2, rows_of, width), jnp.float32),
            pltpu.VMEM((nz * 2, rows_of, width), jnp.float32),
            pltpu.VMEM((nz, 2, rows_of, width), jnp.float32),
            pltpu.VMEM((2, *tile), jnp.float32),
            pltpu.VMEM((3, nz * NC, 1, width), jnp.float32),
            dma((9,)),
            dma((3, nz)),
            dma((3, nz)),
            dma((nz, NY)),
            dma((nz, NY)),
            dma((4 * nx,)),
            dma((4 * nx,)),
            dma((nz,)),
            dma((nz,)),
            dma((3, nz * NC)),
            dma((3, nz * NC)),
        ],
        compiler_params=pltpu.CompilerParams(
            collective_id=0, has_side_effects=True, vmem_limit_bytes=67043328
        ),
    )(
        domain,
        jnp.swapaxes(pattern[0, 0], 1, 2),
        amps[0, 0],
        driver[0, 0],
        virt_energy,
        pair_gap,
        integrals,
    )
    return (new_amps[None, None], rms.reshape(()))


def solution(mesh):
    in_specs = (
        P("blk", "col", None, None, None),
        P("blk", "col", None, None, None),
        P("blk", "col", None, None, None),
        P("blk", "col", None),
        P("blk", "col", None, None),
        P("blk", "col", None),
        P("col", None, None),
    )
    out_specs = (P("blk", "col", None, None, None), P())
    return jax.shard_map(
        per_device, mesh=mesh, in_specs=in_specs, out_specs=out_specs, check_vma=False
    )
```

time: 58.6 us -> 51.9 us (0.89)
  Pallas kernels: 50.4 us -> 47.4 us
  local copies, waits for them, and re-layouts: 4.5 us -> 1.57 us
  other arithmetic: 0.87 us -> 0 us
    pallas_call x1, Pallas kernels: 50.4 us -> 47.4 us  [per_device(): pl.pallas_call(functools.partial(kernel, nz, nx, entries), out_shape=(jax...]
    unnamed x14 -> x1, local copies, waits for them, and re-layouts: 3.9 us -> 1.57 us
    broadcast_in_dim x1 -> x0, other arithmetic: 0.8 us -> none  [per_device(): return (new_amps[None, None], resid_rms)]
where the time goes in v2:
time: 51.9 us; the launch traced here: 51.4 us
  Pallas kernels  47.4 us (91%)
  between operations  2.45 us (5%)
  local copies, waits for them, and re-layouts  1.57 us (3%)
    pallas_call x1, Pallas kernels, per_device(): pl.pallas_call(functools.partial(kernel, nz, nx, entries), out_shape=(jax...  47.4 us
    unnamed x1, local copies, waits for them, and re-layouts  1.57 us

profile of v2, /device:TPU:1, one launch (start us, length us, event | category | flops | bytes accessed | tf_op | source)
XLA Modules:
  0.0 51.4 jit_solution(10265073109957926949)
XLA Ops:
  0.6 47.4 %shard_map.86 = (f32[2,128,128]{2,1,0:T(8,128)}, f32[1,1]{1,0:T(1,128)}) custom-call(s32[1,1,2]{2,1,0:T(1,128)} %domain.1, s32[2,2,32]{2,1,0:T(2,128)} %bitcast.10, bf16[2,128,128]{2,1,0:T(8,128)(2,1)} %bitcast.9, f32[2,128,128]{2,1,0:T(8,128)} %bitcast.7, f32[1,1,2,128]{3,2,1,0:T(2,128)} %energy.1, f32[1,1,2]{2,1,0:T(1,128)} %gap.1, ...), custom_call_target="tpu_custom_call" | custom-call | tf_op jit(solution)/shard_map/pallas_call | solution.py:345
  48.0 1.6 %copy.11 = f32[1,1,2,128,128]{4,3,2,1,0:T(8,128)} copy(f32[1,1,2,128,128]{4,3,2,1,0:T(8,128)} %bitcast.8) | data formatting | bytes 262144

commit v3 on v2

--- a/solution.py
+++ b/solution.py
@@ -43,10 +43,15 @@
     driver_v,
     denom,
     table,
-    h,
+    h_own,
+    h_near,
+    h_far,
+    lanes,
+    ints_out,
     ints,
     idx,
     drv,
+    y_own,
     y_near,
     y_far,
     acc,
@@ -125,15 +130,30 @@
         inside = (across < domain_s[0, 0, q]) & (down < domain_s[0, 0, q])
         held[q] = jnp.where(inside, amps_v[q].astype(f32), 0.0).astype(jnp.bfloat16)
     for q in range(2):
-        h[0, 0, q] = held[q, mine, :]
+        h_own[0, q] = held[q, mine, :]
 
     gets[2].wait()
-    ints[z] = jnp.zeros(ints.shape[1:], jnp.int32)
+    lanes[...] = jnp.zeros_like(lanes)
     places = pattern_v.shape[-1]
     for p in range(2):
         tiles = pattern_v[p]
-        ints[z, 2 * p : 2 * p + 2, 0:places] = jnp.where(tiles < 0, nk, tiles)
-        ints[z, 4 + p : 5 + p, :] = jnp.full((1, width), domain_s[0, 0, p], jnp.int32)
+        lanes[2 * p : 2 * p + 2, 0:places] = jnp.where(tiles < 0, nk, tiles)
+    spread = lanes[...]
+    n = places
+    while n < width:
+        spread = spread + pltpu.roll(spread, n, 1)
+        n *= 2
+    lane = lax.broadcasted_iota(jnp.int32, lanes.shape, 1)
+    sub = lax.broadcasted_iota(jnp.int32, lanes.shape, 0)
+    spread = jnp.where(
+        lane % NY + yh < NY,
+        pltpu.roll(spread, (width - yh) % width, 1),
+        pltpu.roll(spread, (width - yh + NY) % width, 1),
+    )
+    for d in range(nz):
+        turned = pltpu.roll(spread, (width - NY * ((z + d) % nz)) % width, 1)
+        turned = jnp.where(sub == 4, domain_s[0, 0, 0], jnp.where(sub == 5, domain_s[0, 0, 1], turned))
+        ints_out[d] = turned
 
     gets[3].wait()
     gets[4].wait()
@@ -160,17 +180,24 @@
 
     order = near_first(nz)
     slot = {d: i for i, d in enumerate([0] + order)}
+    near = h_near.shape[0]
+
+    def piece(d, dy):
+        if dy == 0:
+            return h_own.at[slot[d]]
+        if slot[d] < near:
+            return h_near.at[slot[d], dy - 1]
+        return h_far.at[slot[d] - near, dy - 1]
 
     for d in far_first(nz):
-        send(held.at[:, their_rows(d), :], h.at[slot[d], 0], z_send.at[0, d], z_recv.at[0, d], at_z(d))
+        send(held.at[:, their_rows(d), :], piece(d, 0), z_send.at[0, d], z_recv.at[0, d], at_z(d))
 
     def piece_out(d):
-        piece = h.at[slot[d], 0]
         for dy in (2, 1, 3):
-            send(piece, h.at[slot[d], dy], y_send.at[d, dy], y_recv.at[d, dy], at_yh(dy))
+            send(piece(d, 0), piece(d, dy), y_send.at[d, dy], y_recv.at[d, dy], at_yh(dy))
 
     def piece_from_z(d):
-        arrived(h.at[slot[d], 0], z_send.at[0, d], z_recv.at[0, d])
+        arrived(piece(d, 0), z_send.at[0, d], z_recv.at[0, d])
         piece_out(d)
 
     def owner(dx, other, far_core):
@@ -205,15 +232,15 @@
     piece_out(0)
     unit_to_sibling(0, 0)
     for d in far_first(nz):
-        send(ints.at[z], ints.at[z], z_send.at[1, d], z_recv.at[1, d], at_z(d))
+        send(ints_out.at[d], ints.at[z], z_send.at[1, d], z_recv.at[1, d], at_z(d))
     gets[5].wait()
     for d in far_first(nz):
         send(driver_v.at[:, their_rows(d), :], drv.at[z], z_send.at[2, d], z_recv.at[2, d], at_z(d))
     for p in range(2):
         drv[z, p] = driver_v[p, mine, :]
-    acc[...] = jnp.zeros_like(acc)
-    y_near[nk] = jnp.zeros(y_near.shape[1:], f32)
-    y_far[nk] = jnp.zeros(y_far.shape[1:], f32)
+    ints[z] = ints_out[0]
+    for y in (y_own, y_near, y_far):
+        y[:, nk] = jnp.zeros((y.shape[0], *y.shape[2:]), f32)
 
     for d in order[:4]:
         piece_from_z(d)
@@ -239,47 +266,58 @@
         own = jnp.broadcast_to(energy_v[0, 0, p : p + 1, :], (width, width))
         turned = jnp.sum(jnp.where(across == down, own, 0.0), axis=1, keepdims=True)
         denom[p] = turned + own + gap_s[0, 0, p]
-    for d in near_first(nx):
-        unit_from_x(d, 1)
+
+    def rows_of(h):
+        count = h.size // width
+        return h[...].reshape(count, width)
+
+    def products(lhs, y, dx, other, far_core):
+        o = owner(dx, other, far_core)
+        both = jnp.dot(lhs, table[o], preferred_element_type=f32)
+        y[:, 2 * o] = both[:, :width].reshape(y.shape[0], rows, width)
+        y[:, 2 * o + 1] = both[:, width:].reshape(y.shape[0], rows, width)
+
+    def add_up(pieces, y, first):
+        def step(zo, carry):
+            for p in range(2):
+                total = None if first else acc[zo * 2 + p]
+                for i, (d, dy) in enumerate(pieces):
+                    place = ((nz - d) % nz) * NY + (NY - dy) % NY
+                    for q in range(2):
+                        k = idx[zo, p * 2 + q, place]
+                        term = y[i * 2 + q, k]
+                        total = term if total is None else total + term
+                acc[zo * 2 + p] = total
+            return carry
+
+        lax.fori_loop(0, nz, step, 0)
+
+    own_units = [(0, 0), (0, 1)] + [(dx, 0) for dx in near_first(nx)]
+    late_units = [(dx, 1) for dx in near_first(nx)]
+    lhs = rows_of(h_own)
+    for dx, other in own_units:
+        products(lhs, y_own, dx, other, 0)
+    for dx, other in late_units:
+        unit_from_x(dx, other)
+    for dx, other in late_units:
+        products(lhs, y_own, dx, other, 0)
+    units = [(dx, other, 0) for dx, other in own_units + late_units]
+    for dx, other in own_units + late_units:
+        unit_in(dx, other, 1)
+        products(lhs, y_own, dx, other, 1)
+        units.append((dx, other, 1))
     get_idx.wait()
-
-    def pieces_in(ds):
-        for d in ds:
-            for dy in (1, 3, 2):
-                arrived(h.at[slot[d], dy], y_send.at[d, dy], y_recv.at[d, dy])
-
-    def couple(ds, y, wait_units):
-        first, count = slot[ds[0]], len(ds)
-        lhs = h[first : first + count].reshape(count * NY * 2 * rows, width)
-        for far_core in range(2):
-            for other in range(2):
-                for dx in [0] + near_first(nx):
-                    if wait_units and far_core:
-                        unit_in(dx, other, 1)
-                    o = owner(dx, other, far_core)
-                    both = jnp.dot(lhs, table[o], preferred_element_type=f32)
-                    y[2 * o] = both[:, :width].reshape(count * NY * 2, rows, width)
-                    y[2 * o + 1] = both[:, width:].reshape(count * NY * 2, rows, width)
-        behind = [[((z - d + nz) % nz) * NY + (yh - dy + NY) % NY for dy in range(NY)] for d in ds]
-
-        def add_up(g, carry):
-            zo, p = g // 2, g % 2
-            total = acc[g]
-            for i in range(count):
-                for dy in range(NY):
-                    for q in range(2):
-                        k = idx[zo, p * 2 + q, behind[i][dy]]
-                        total = total + y[k, (i * NY + dy) * 2 + q]
-            acc[g] = total
-            return carry
-
-        lax.fori_loop(0, nz * 2, add_up, 0)
-
-    near = [0] + order[:4]
-    pieces_in(near)
-    couple(near, y_near, True)
-    pieces_in(order[4:])
-    couple(order[4:], y_far, False)
+    add_up([(d, 0) for d in [0] + order], y_own, True)
+
+    ahead = [0] + order
+    for h, y, ds in ((h_near, y_near, ahead[:near]), (h_far, y_far, ahead[near:])):
+        pieces = [(d, dy) for d in ds for dy in range(1, NY)]
+        for d, dy in pieces:
+            arrived(piece(d, dy), y_send.at[d, dy], y_recv.at[d, dy])
+        lhs = rows_of(h)
+        for n in units:
+            products(lhs, y, *n)
+        add_up(pieces, y, False)
 
     for d in order:
         arrived(drv.at[(z - d + nz) % nz], z_send.at[2, d], z_recv.at[2, d])
@@ -323,10 +361,10 @@
         arrived(home.at[:, theirs, :], r_send.at[d], r_recv.at[d])
     for p in range(2):
         amps_out[p] = held[p].astype(f32) + home[p] / denom[p]
+    for copy in sends:
+        copy.wait_send()
     total = stage_in(2, [(x - d + nx) % nx for d in far_first(nx)])
     rms_out[0, 0] = jnp.max(jnp.sqrt(jnp.full((8, width), jnp.sum(total) / entries, f32)))
-    for copy in sends:
-        copy.wait_send()
 
 
 def per_device(amps, driver, pattern, domain, virt_energy, pair_gap, integrals):
@@ -342,6 +380,15 @@
     dma = pltpu.SemaphoreType.DMA
     in_hbm = pl.BlockSpec(memory_space=pltpu.HBM)
     tile = (width, width)
+    operands = (
+        domain,
+        jnp.swapaxes(pattern[0, 0], 1, 2),
+        amps[0, 0],
+        driver[0, 0],
+        virt_energy,
+        pair_gap,
+        integrals,
+    )
     new_amps, rms = pl.pallas_call(
         functools.partial(kernel, nz, nx, entries),
         out_shape=(
@@ -360,12 +407,17 @@
             pltpu.VMEM((2, *tile), jnp.float32),
             pltpu.VMEM((2, *tile), jnp.float32),
             pltpu.VMEM((owners, width, 2 * width), jnp.bfloat16),
-            pltpu.VMEM((nz, NY, 2, rows_of, width), jnp.bfloat16),
+            pltpu.VMEM((nz, 2, rows_of, width), jnp.bfloat16),
+            pltpu.VMEM((near, NY - 1, 2, rows_of, width), jnp.bfloat16),
+            pltpu.VMEM((nz - near, NY - 1, 2, rows_of, width), jnp.bfloat16),
+            pltpu.VMEM((8, width), jnp.int32),
+            pltpu.VMEM((nz, 8, width), jnp.int32),
             pltpu.VMEM((nz, 8, width), jnp.int32),
             pltpu.SMEM((nz, 8, width), jnp.int32),
             pltpu.VMEM((nz, 2, rows_of, width), jnp.float32),
-            pltpu.VMEM((nk + 1, near * NY * 2, rows_of, width), jnp.float32),
-            pltpu.VMEM((nk + 1, (nz - near) * NY * 2, rows_of, width), jnp.float32),
+            pltpu.VMEM((nz * 2, nk + 1, rows_of, width), jnp.float32),
+            pltpu.VMEM((near * (NY - 1) * 2, nk + 1, rows_of, width), jnp.float32),
+            pltpu.VMEM(((nz - near) * (NY - 1) * 2, nk + 1, rows_of, width), jnp.float32),
             pltpu.VMEM((nz * 2, rows_of, width), jnp.float32),
             pltpu.VMEM((nz, 2, rows_of, width), jnp.float32),
             pltpu.VMEM((2, *tile), jnp.float32),
@@ -383,16 +435,10 @@
             dma((3, nz * NC)),
         ],
         compiler_params=pltpu.CompilerParams(
-            collective_id=0, has_side_effects=True, vmem_limit_bytes=67043328
+            collective_id=0, has_side_effects=True, vmem_limit_bytes=40 * 1024 * 1024
         ),
     )(
-        domain,
-        jnp.swapaxes(pattern[0, 0], 1, 2),
-        amps[0, 0],
-        driver[0, 0],
-        virt_energy,
-        pair_gap,
-        integrals,
+        *(pltpu.with_memory_space_constraint(a, pltpu.HBM) for a in operands)
     )
     return (new_amps[None, None], rms.reshape(()))
 

time: 51.9 us -> 47.7 us (0.919)
  Pallas kernels: 47.4 us -> 44.4 us
  local copies, waits for them, and re-layouts: 1.57 us -> 0.66 us
    pallas_call x1, Pallas kernels: 47.4 us -> 44.4 us  [per_device(): pl.pallas_call(functools.partial(kernel, nz, nx, entries), out_shape=(jax...]
    unnamed x1, local copies, waits for them, and re-layouts: 1.57 us -> 0.66 us
where the time goes in v3:
time: 47.7 us; the launch traced here: 47.4 us
  Pallas kernels  44.4 us (93%)
  between operations  2.33 us (5%)
  local copies, waits for them, and re-layouts  0.66 us (1%)
    pallas_call x1, Pallas kernels, per_device(): pl.pallas_call(functools.partial(kernel, nz, nx, entries), out_shape=(jax...  44.4 us

profile of v3, /device:TPU:1, one launch (start us, length us, event | category | flops | bytes accessed | tf_op | source)
XLA Modules:
  0.0 47.4 jit_solution(1653707954093254911)
XLA Ops:
  0.6 44.4 %shard_map.86 = (f32[2,128,128]{2,1,0:T(8,128)S(1)}, f32[1,1]{1,0:T(1,128)}) custom-call(s32[1,1,2]{2,1,0:T(1,128)} %domain.1, s32[2,2,32]{2,1,0:T(2,128)} %bitcast.10, bf16[2,128,128]{2,1,0:T(8,128)(2,1)} %bitcast.9, f32[2,128,128]{2,1,0:T(8,128)} %bitcast.8, f32[1,1,2,128]{3,2,1,0:T(2,128)} %energy.1, f32[1,1,2]{2,1,0:T(1,128)} %gap.1, ...), custom_call_target="tpu_custom_call" | custom-call | tf_op jit(solution)/shard_map/pallas_call | solution.py:392
  45.1 0.7 %copy.11 = f32[1,1,2,128,128]{4,3,2,1,0:T(8,128)} copy(f32[1,1,2,128,128]{4,3,2,1,0:T(8,128)S(1)} %bitcast.7) | data formatting | bytes 262144

commit v4 on v3

--- a/solution.py
+++ b/solution.py
@@ -65,6 +65,10 @@
     y_recv,
     t_send,
     t_recv,
+    o_send,
+    o_recv,
+    p_send,
+    p_recv,
     r_send,
     r_recv,
     m_send,
@@ -95,7 +99,8 @@
     def at_zc(d, e):
         return (((z + d) % nz) * NY + yh, (x * NL + yl) * NC + (core + e) % NC)
 
-    over = (blk, (x * NL + 1 - yl) * NC + core)
+    beyond = (yh + 2 * yl - 1 + NY) % NY
+    over = [(b, (x * NL + 1 - yl) * NC + core) for b in (blk, z * NY + beyond)]
     sibling = (blk, (x * NL + yl) * NC + 1 - core)
     zc_far = [(d, e) for d in far_first(nz) for e in range(NC)] + [(0, 1)]
 
@@ -210,10 +215,21 @@
     def kind(dx, other, far_core=0):
         return dx + nx * other + 2 * nx * far_core
 
-    def unit_along_x(other):
-        n = unit(0, other)
+    half = width // 2
+
+    def part(dx, other, i):
+        return unit(dx, other).at[pl.ds(i * half, half), :]
+
+    def unit_along_x():
+        n = unit(0, 0)
         for d in far_first(nx):
-            send(n, n, t_send.at[kind(d, other)], t_recv.at[kind(d, other)], at_x(d))
+            send(n, n, t_send.at[kind(d, 0)], t_recv.at[kind(d, 0)], at_x(d))
+
+    def part_along_x(i):
+        n = part(0, 1, i)
+        arrived(n, o_send.at[i], o_recv.at[i])
+        for d in far_first(nx):
+            send(n, n, p_send.at[d, i], p_recv.at[d, i], at_x(d))
 
     def unit_to_sibling(dx, other):
         n = unit(dx, other)
@@ -224,11 +240,16 @@
         arrived(unit(dx, other, far_core), t_send.at[n], t_recv.at[n])
 
     def unit_from_x(dx, other):
-        unit_in(dx, other)
+        if other:
+            for i in range(2):
+                arrived(part(dx, 1, i), p_send.at[dx, i], p_recv.at[dx, i])
+        else:
+            unit_in(dx, 0)
         unit_to_sibling(dx, other)
 
-    send(unit(0, 0), unit(0, 0), t_send.at[kind(0, 1)], t_recv.at[kind(0, 1)], over)
-    unit_along_x(0)
+    for i, device in enumerate(over):
+        send(part(0, 0, i), part(0, 0, i), o_send.at[i], o_recv.at[i], device)
+    unit_along_x()
     piece_out(0)
     unit_to_sibling(0, 0)
     for d in far_first(nz):
@@ -244,8 +265,8 @@
 
     for d in order[:4]:
         piece_from_z(d)
-    unit_in(0, 1)
-    unit_along_x(1)
+    part_along_x(0)
+    part_along_x(1)
     unit_to_sibling(0, 1)
     for d in order[4:6]:
         piece_from_z(d)
@@ -292,32 +313,46 @@
 
         lax.fori_loop(0, nz, step, 0)
 
-    own_units = [(0, 0), (0, 1)] + [(dx, 0) for dx in near_first(nx)]
-    late_units = [(dx, 1) for dx in near_first(nx)]
-    lhs = rows_of(h_own)
-    for dx, other in own_units:
-        products(lhs, y_own, dx, other, 0)
-    for dx, other in late_units:
-        unit_from_x(dx, other)
-    for dx, other in late_units:
-        products(lhs, y_own, dx, other, 0)
-    units = [(dx, other, 0) for dx, other in own_units + late_units]
-    for dx, other in own_units + late_units:
-        unit_in(dx, other, 1)
-        products(lhs, y_own, dx, other, 1)
-        units.append((dx, other, 1))
-    get_idx.wait()
-    add_up([(d, 0) for d in [0] + order], y_own, True)
-
+    early = [(0, 0), (0, 1)] + [(dx, 0) for dx in near_first(nx)]
+    late = [(dx, 1) for dx in near_first(nx)]
     ahead = [0] + order
-    for h, y, ds in ((h_near, y_near, ahead[:near]), (h_far, y_far, ahead[near:])):
-        pieces = [(d, dy) for d in ds for dy in range(1, NY)]
+    pieces_near = [(d, dy) for d in ahead[:near] for dy in range(1, NY)]
+    pieces_far = [(d, dy) for d in ahead[near:] for dy in range(1, NY)]
+
+    def pieces_in(pieces):
         for d, dy in pieces:
             arrived(piece(d, dy), y_send.at[d, dy], y_recv.at[d, dy])
-        lhs = rows_of(h)
-        for n in units:
-            products(lhs, y, *n)
-        add_up(pieces, y, False)
+
+    own = rows_of(h_own)
+    for n in early:
+        products(own, y_own, *n, 0)
+    for n in early:
+        unit_in(*n, 1)
+        products(own, y_own, *n, 1)
+    for n in late:
+        unit_from_x(*n)
+    for n in late:
+        products(own, y_own, *n, 0)
+    pieces_in(pieces_near)
+    beside = rows_of(h_near)
+    for far_core in range(2):
+        for n in early:
+            products(beside, y_near, *n, far_core)
+    for n in late:
+        products(beside, y_near, *n, 0)
+    for n in late:
+        unit_in(*n, 1)
+        products(own, y_own, *n, 1)
+        products(beside, y_near, *n, 1)
+    get_idx.wait()
+    add_up([(d, 0) for d in ahead], y_own, True)
+    add_up(pieces_near, y_near, False)
+    pieces_in(pieces_far)
+    beyond_rows = rows_of(h_far)
+    for far_core in range(2):
+        for n in early + late:
+            products(beyond_rows, y_far, *n, far_core)
+    add_up(pieces_far, y_far, False)
 
     for d in order:
         arrived(drv.at[(z - d + nz) % nz], z_send.at[2, d], z_recv.at[2, d])
@@ -376,7 +411,7 @@
     owners = lax.axis_size("col")
     nk = owners * integrals.shape[0]
     entries = float(lax.axis_size("blk") * owners * per_block * width * width)
-    near = 5
+    near = 3
     dma = pltpu.SemaphoreType.DMA
     in_hbm = pl.BlockSpec(memory_space=pltpu.HBM)
     tile = (width, width)
@@ -429,6 +464,10 @@
             dma((nz, NY)),
             dma((4 * nx,)),
             dma((4 * nx,)),
+            dma((2,)),
+            dma((2,)),
+            dma((nx, 2)),
+            dma((nx, 2)),
             dma((nz,)),
             dma((nz,)),
             dma((3, nz * NC)),

time: 47.7 us -> 47.1 us (0.987)
  Pallas kernels: 44.4 us -> 43.7 us
    pallas_call x1, Pallas kernels: 44.4 us -> 43.7 us  [per_device(): pl.pallas_call(functools.partial(kernel, nz, nx, entries), out_shape=(jax...]
where the time goes in v4:
time: 47.1 us; the launch traced here: 46.7 us
  Pallas kernels  43.7 us (93%)
  between operations  2.33 us (5%)
  local copies, waits for them, and re-layouts  0.66 us (1%)
    pallas_call x1, Pallas kernels, per_device(): pl.pallas_call(functools.partial(kernel, nz, nx, entries), out_shape=(jax...  43.7 us

profile of v4, /device:TPU:1, one launch (start us, length us, event | category | flops | bytes accessed | tf_op | source)
XLA Modules:
  0.0 46.7 jit_solution(15737558551354541713)
XLA Ops:
  0.6 43.7 %shard_map.86 = (f32[2,128,128]{2,1,0:T(8,128)S(1)}, f32[1,1]{1,0:T(1,128)}) custom-call(s32[1,1,2]{2,1,0:T(1,128)} %domain.1, s32[2,2,32]{2,1,0:T(2,128)} %bitcast.10, bf16[2,128,128]{2,1,0:T(8,128)(2,1)} %bitcast.9, f32[2,128,128]{2,1,0:T(8,128)} %bitcast.8, f32[1,1,2,128]{3,2,1,0:T(2,128)} %energy.1, f32[1,1,2]{2,1,0:T(1,128)} %gap.1, ...), custom_call_target="tpu_custom_call" | custom-call | tf_op jit(solution)/shard_map/pallas_call | solution.py:427
  44.4 0.7 %copy.11 = f32[1,1,2,128,128]{4,3,2,1,0:T(8,128)} copy(f32[1,1,2,128,128]{4,3,2,1,0:T(8,128)S(1)} %bitcast.7) | data formatting | bytes 262144

commit v5 on v4

--- a/solution.py
+++ b/solution.py
@@ -99,15 +99,22 @@
     def at_zc(d, e):
         return (((z + d) % nz) * NY + yh, (x * NL + yl) * NC + (core + e) % NC)
 
+    def at_yx(d, e):
+        place = (yh * NL + yl + d) % (NY * NL)
+        return (z * NY + place // NL, (((x + e) % nx) * NL + place % NL) * NC + core)
+
     beyond = (yh + 2 * yl - 1 + NY) % NY
     over = [(b, (x * NL + 1 - yl) * NC + core) for b in (blk, z * NY + beyond)]
     sibling = (blk, (x * NL + yl) * NC + 1 - core)
     zc_far = [(d, e) for d in far_first(nz) for e in range(NC)] + [(0, 1)]
+    yx_far = sorted(
+        [(d, e) for d in range(NY * NL) for e in range(nx) if d or e],
+        key=lambda n: -min(n[0], NY * NL - n[0]) - min(n[1], nx - n[1]),
+    )
 
     barrier = pltpu.get_barrier_semaphore()
     greeted = [at_zc(d, e) for d, e in zc_far]
-    greeted += [at_y(d) for d in far_first(NY * NL)]
-    greeted += [at_x(d) for d in far_first(nx)]
+    greeted += [at_yx(d, e) for d, e in yx_far]
     for device in greeted:
         pl.semaphore_signal(barrier, inc=1, device_id=device, device_id_type=MESH)
 
@@ -388,9 +395,7 @@
     for p in range(2):
         home[p, mine, :] = back[z, p]
     total = stage_in(0, [((z - d + nz) % nz) * NC + (core + e) % NC for d, e in zc_far])
-    stage_out(1, yy, [at_y(d) for d in far_first(ny)], total)
-    total = stage_in(1, [(yy - d + ny) % ny for d in far_first(ny)])
-    stage_out(2, x, [at_x(d) for d in far_first(nx)], total)
+    stage_out(1, yy * nx + x, [at_yx(d, e) for d, e in yx_far], total)
     for d in order:
         theirs = pl.ds(pl.multiple_of(((z - d + nz) % nz) * rows, rows), rows)
         arrived(home.at[:, theirs, :], r_send.at[d], r_recv.at[d])
@@ -398,7 +403,7 @@
         amps_out[p] = held[p].astype(f32) + home[p] / denom[p]
     for copy in sends:
         copy.wait_send()
-    total = stage_in(2, [(x - d + nx) % nx for d in far_first(nx)])
+    total = stage_in(1, [((yy - d + ny) % ny) * nx + (x - e + nx) % nx for d, e in yx_far])
     rms_out[0, 0] = jnp.max(jnp.sqrt(jnp.full((8, width), jnp.sum(total) / entries, f32)))
 
 
@@ -412,6 +417,7 @@
     nk = owners * integrals.shape[0]
     entries = float(lax.axis_size("blk") * owners * per_block * width * width)
     near = 3
+    sums = max(nz * NC, NY * NL * nx)
     dma = pltpu.SemaphoreType.DMA
     in_hbm = pl.BlockSpec(memory_space=pltpu.HBM)
     tile = (width, width)
@@ -456,7 +462,7 @@
             pltpu.VMEM((nz * 2, rows_of, width), jnp.float32),
             pltpu.VMEM((nz, 2, rows_of, width), jnp.float32),
             pltpu.VMEM((2, *tile), jnp.float32),
-            pltpu.VMEM((3, nz * NC, 1, width), jnp.float32),
+            pltpu.VMEM((2, sums, 1, width), jnp.float32),
             dma((9,)),
             dma((3, nz)),
             dma((3, nz)),
@@ -470,8 +476,8 @@
             dma((nx, 2)),
             dma((nz,)),
             dma((nz,)),
-            dma((3, nz * NC)),
-            dma((3, nz * NC)),
+            dma((2, sums)),
+            dma((2, sums)),
         ],
         compiler_params=pltpu.CompilerParams(
             collective_id=0, has_side_effects=True, vmem_limit_bytes=40 * 1024 * 1024

time: 47.1 us -> 46.1 us (0.979)
  Pallas kernels: 43.7 us -> 43 us
    pallas_call x1, Pallas kernels: 43.7 us -> 43 us  [per_device(): pl.pallas_call(functools.partial(kernel, nz, nx, entries), out_shape=(jax...]
where the time goes in v5:
time: 46.1 us; the launch traced here: 46 us
  Pallas kernels  43 us (93%)
  between operations  2.33 us (5%)
  local copies, waits for them, and re-layouts  0.66 us (1%)
    pallas_call x1, Pallas kernels, per_device(): pl.pallas_call(functools.partial(kernel, nz, nx, entries), out_shape=(jax...  43 us

profile of v5, /device:TPU:1, one launch (start us, length us, event | category | flops | bytes accessed | tf_op | source)
XLA Modules:
  0.0 46.0 jit_solution(9897306647480108039)
XLA Ops:
  0.6 43.0 %shard_map.86 = (f32[2,128,128]{2,1,0:T(8,128)S(1)}, f32[1,1]{1,0:T(1,128)}) custom-call(s32[1,1,2]{2,1,0:T(1,128)} %domain.1, s32[2,2,32]{2,1,0:T(2,128)} %bitcast.10, bf16[2,128,128]{2,1,0:T(8,128)(2,1)} %bitcast.9, f32[2,128,128]{2,1,0:T(8,128)} %bitcast.8, f32[1,1,2,128]{3,2,1,0:T(2,128)} %energy.1, f32[1,1,2]{2,1,0:T(1,128)} %gap.1, ...), custom_call_target="tpu_custom_call" | custom-call | tf_op jit(solution)/shard_map/pallas_call | solution.py:433
  43.7 0.7 %copy.11 = f32[1,1,2,128,128]{4,3,2,1,0:T(8,128)} copy(f32[1,1,2,128,128]{4,3,2,1,0:T(8,128)S(1)} %bitcast.7) | data formatting | bytes 262144

commit v6 on v5

--- a/solution.py
+++ b/solution.py
@@ -114,7 +114,8 @@
 
     barrier = pltpu.get_barrier_semaphore()
     greeted = [at_zc(d, e) for d, e in zc_far]
-    greeted += [at_yx(d, e) for d, e in yx_far]
+    greeted += [at_y(d) for d in far_first(NY * NL)]
+    greeted += [at_x(d) for d in far_first(nx)]
     for device in greeted:
         pl.semaphore_signal(barrier, inc=1, device_id=device, device_id_type=MESH)
 

time: 46.1 us -> 45.9 us (level)
  no operation moved by 1% of the time
where the time goes in v6:
time: 45.9 us; the launch traced here: 45.7 us
  Pallas kernels  42.8 us (93%)
  between operations  2.33 us (5%)
  local copies, waits for them, and re-layouts  0.66 us (1%)
    pallas_call x1, Pallas kernels, per_device(): pl.pallas_call(functools.partial(kernel, nz, nx, entries), out_shape=(jax...  42.8 us

profile of v6, /device:TPU:1, one launch (start us, length us, event | category | flops | bytes accessed | tf_op | source)
XLA Modules:
  0.0 45.7 jit_solution(1697440761787810575)
XLA Ops:
  0.6 42.8 %shard_map.86 = (f32[2,128,128]{2,1,0:T(8,128)S(1)}, f32[1,1]{1,0:T(1,128)}) custom-call(s32[1,1,2]{2,1,0:T(1,128)} %domain.1, s32[2,2,32]{2,1,0:T(2,128)} %bitcast.10, bf16[2,128,128]{2,1,0:T(8,128)(2,1)} %bitcast.9, f32[2,128,128]{2,1,0:T(8,128)} %bitcast.8, f32[1,1,2,128]{3,2,1,0:T(2,128)} %energy.1, f32[1,1,2]{2,1,0:T(1,128)} %gap.1, ...), custom_call_target="tpu_custom_call" | custom-call | tf_op jit(solution)/shard_map/pallas_call | solution.py:434
  43.4 0.7 %copy.11 = f32[1,1,2,128,128]{4,3,2,1,0:T(8,128)} copy(f32[1,1,2,128,128]{4,3,2,1,0:T(8,128)S(1)} %bitcast.7) | data formatting | bytes 262144
